TPU v7x, 128 devices: a whole 4x4x4 slice. The times are simulated.
128 devices in a mesh: row: 8 (over z, x_hi), col: 16 (over x_lo, y, core).
Axes of the slice: x: 4 (x_hi: 2, x_lo: 2; x = x_hi * 2 + x_lo), y: 4, z: 4, core: 2. Of those that a mesh axis runs over, the one named last changes fastest.
Arguments:
- embeddings: bfloat16 [32768, 768], P(('row', 'col'))
- spread: bfloat16 [32768], P(('row', 'col')), may hold values from 1 to 16
- features: bfloat16 [32768, 256], P(('row', 'col')), may hold values from -160 to 160
- block_list: int32 [256], replicated, may hold values from 0 to 63
- list_pairs: int32 [64, 64], replicated, may hold values from 0 to 1, as said below
Outputs:
- smoothed: float32 [32768, 256], P(('row', 'col'))
Inputs may be any that keep to these rules, and one draw needn't show every extreme that they name: `list_pairs`: symmetric, with ones on the diagonal.
All inputs are finite; a program needn't handle non-finite values.
Results may differ from a plain program's by a relative error of at most 0.0029.
Values may be sent and summed in bfloat16 or wider, within the bound.
A program may use at most 64 MiB of HBM per device.

v0:
```python
import math
import jax
import jax.numpy as jnp
from jax import lax
from jax.sharding import PartitionSpec as P

BLK = 128
LISTS = 64


def active_table(block_list, list_pairs, row_blocks, col_blocks):
    count = block_list.shape[0]
    lists_onehot = (block_list[:, None] == jnp.arange(LISTS, dtype=jnp.int32)[None, :]).astype(
        jnp.float32
    )
    pair_table = list_pairs.astype(jnp.float32)
    row_select = (row_blocks[:, None] == jnp.arange(count, dtype=jnp.int32)[None, :]).astype(
        jnp.float32
    )
    col_select = (col_blocks[:, None] == jnp.arange(count, dtype=jnp.int32)[None, :]).astype(
        jnp.float32
    )
    row_onehot = jnp.dot(row_select, lists_onehot, precision=lax.Precision.HIGHEST)
    col_onehot = jnp.dot(col_select, lists_onehot, precision=lax.Precision.HIGHEST)
    joined = jnp.dot(row_onehot, pair_table, precision=lax.Precision.HIGHEST)
    return jnp.dot(joined, col_onehot.T, precision=lax.Precision.HIGHEST)


def shards(embeddings, spread, features, block_list, list_pairs):
    rows_x, rows_beta = (
        lax.all_gather(embeddings, "col", axis=0, tiled=True),
        lax.all_gather(spread, "col", axis=0, tiled=True),
    )
    cols_x, cols_beta, cols_feat = (
        lax.all_gather(embeddings, "row", axis=0, tiled=True),
        lax.all_gather(spread, "row", axis=0, tiled=True),
        lax.all_gather(features, "row", axis=0, tiled=True),
    )
    own_count = embeddings.shape[0]
    col_size = lax.axis_size("col")
    row_index = lax.axis_index("row")
    col_index = lax.axis_index("col")
    total_rows = rows_x.shape[0]
    total_cols = cols_x.shape[0]
    row_ids = row_index * total_rows + jnp.arange(total_rows, dtype=jnp.int32)
    local_index = jnp.arange(total_cols, dtype=jnp.int32)
    col_ids = (
        local_index // own_count * col_size + col_index
    ) * own_count + local_index % own_count
    active = active_table(block_list, list_pairs, row_ids[::BLK] // BLK, col_ids[::BLK] // BLK)
    col_blocks = active.shape[1]
    row_norm = jnp.sum(jnp.square(rows_x.astype(jnp.float32)), axis=1)
    col_norm = jnp.sum(jnp.square(cols_x.astype(jnp.float32)), axis=1)
    row_bw = rows_beta.astype(jnp.float32)
    col_bw = cols_beta.astype(jnp.float32)

    def block_terms(start, size):
        row_emb = lax.dynamic_slice_in_dim(rows_x, start, size, 0)
        norm_part = lax.dynamic_slice_in_dim(row_norm, start, size, 0)
        beta_part = lax.dynamic_slice_in_dim(row_bw, start, size, 0)
        ids_part = lax.dynamic_slice_in_dim(row_ids, start, size, 0)
        inner = lax.dot_general(
            row_emb, cols_x, (((1,), (1,)), ((), ())), preferred_element_type=jnp.float32
        )
        dist = norm_part[:, None] + col_norm[None, :] - 2.0 * inner
        active_part = lax.dynamic_slice_in_dim(active, start // BLK, size // BLK, 0)
        expanded = jnp.broadcast_to(
            active_part[:, None, :, None], (size // BLK, BLK, col_blocks, BLK)
        )
        mask = expanded.reshape(size, total_cols) * (ids_part[:, None] != col_ids[None, :]).astype(
            jnp.float32
        )
        near = mask * jnp.exp(-beta_part[:, None] * dist)
        return (mask, dist, near)

    block_rows = math.gcd(total_rows, 512)
    starts = jnp.arange(total_rows // block_rows, dtype=jnp.int32) * block_rows
    row_partial = lax.map(
        lambda start: jnp.sum(block_terms(start, block_rows)[2], axis=1), starts
    ).reshape(total_rows)
    row_totals = lax.psum(row_partial, "col")
    own_totals = lax.dynamic_slice_in_dim(row_totals, col_index * own_count, own_count, 0)
    col_totals = lax.all_gather(own_totals, "row", axis=0, tiled=True)
    size = math.gcd(total_rows, 512)

    def one_block(begin):
        mask, dist, near = block_terms(begin, size)
        far = mask * jnp.exp(-col_bw[None, :] * dist)
        total_part = lax.dynamic_slice_in_dim(row_totals, begin, size, 0)
        weight = ((near / total_part[:, None] + far / col_totals[None, :]) * 0.5).astype(
            jnp.bfloat16
        )
        return jnp.dot(weight, cols_feat, preferred_element_type=jnp.float32)

    begins = 0 + jnp.arange(total_rows // size, dtype=jnp.int32) * size
    partial_out = lax.map(one_block, begins).reshape(total_rows, cols_feat.shape[1])
    summed = lax.psum(partial_out, "col")
    return lax.dynamic_slice_in_dim(summed, col_index * own_count, own_count, 0)


def solution(mesh):
    return jax.shard_map(
        shards,
        mesh=mesh,
        in_specs=(P(("row", "col"), None), P(("row", "col")), P(("row", "col"), None), P(), P()),
        out_specs=P(("row", "col"), None),
        check_vma=False,
    )
```

profile of v0, /device:TPU:1, one launch (start us, length us, event | category | flops | bytes accessed | tf_op | source)
XLA Modules:
  0.0 548.1 jit_solution(9659464464459559050)
XLA Ops:
  6.5 0.7 all-gather.9.cloned.1.call-update
  7.3 0.7 all-gather.7.cloned.1.call-update
  8.1 0.7 all-gather.11.cloned.1.call-update
  8.8 0.7 reshape.44
  9.5 21.2 %all-gather = bf16[16,1,256]{2,1,0:T(2,128)(2,1)S(1)} all-gather(bf16[1,1,256]{2,1,0:T(2,128)(2,1)S(1)} %reshape.44), channel_id=1, replica_groups=mesh['row'=8,'col'=16] {'col'}, dimensions={0}, use_global_device_ids=true | all-gather | bytes 8704 | tf_op jit(solution)/shard_map/all_gather | solution.py:32
  30.6 20.6 %all-gather.1 = bf16[8,1,256]{2,1,0:T(2,128)(2,1)S(1)} all-gather(bf16[1,1,256]{2,1,0:T(2,128)(2,1)S(1)} %reshape.44), channel_id=1, replica_groups=mesh['row'=8,'col'=16] {'row'}, dimensions={0}, use_global_device_ids=true | all-gather | bytes 4608 | tf_op jit(solution)/shard_map/all_gather | solution.py:36
  51.5 0.9 fusion.40
  52.4 0.9 fusion.41
  53.3 0.9 fusion.44
  54.4 21.0 %all-gather.9.cloned.1.call-done = bf16[2048,768]{1,0:T(8,128)(2,1)} async-done(((bf16[256,768]{1,0:T(8,128)(2,1)}), bf16[2048,768]{1,0:T(8,128)(2,1)}) %all-gather.9.cloned.1.call-update) | async-done | bytes 3145744 | tf_op jit(solution)/shard_map/all_gather | solution.py:35
  75.3 2.7 multiply_reduce_fusion.1
  78.1 39.8 %all-gather.7.cloned.1.call-done = bf16[4096,768]{1,0:T(8,128)(2,1)} async-done(((bf16[256,768]{1,0:T(8,128)(2,1)}), bf16[4096,768]{1,0:T(8,128)(2,1)}) %all-gather.7.cloned.1.call-update) | async-done | bytes 6291472 | tf_op jit(solution)/shard_map/all_gather | solution.py:31
  117.9 4.1 multiply_reduce_fusion
  122.0 102.0 %while.26 = (s32[]{:T(128)}, f32[8,512]{1,0:T(8,128)S(1)}, s32[8]{0:T(128)S(1)}, s32[4096]{0:T(1024)S(1)}, f32[32,16]{1,0:T(8,128)S(1)}, /*index=5*/f32[4096]{0:...) while((s32[]{:T(128)}, f32[8,512]{1,0:T(8,128)S(1)}, ...), condition=%wide.region_4.5_spmd.clone, body=%wide.region_2.4_spmd.clone.sunk | while | flops 1619034112 | bytes 12371102 | solution.py:78
  122.0 0.6 dynamic_slice.126
  125.1 2.4 broadcast_in_dim.65
  129.0 5.8 %fusion.78 = f32[512]{0:T(512)S(1)} fusion(f32[64,8,16,128]{3,2,1,0:T(8,128)} %bitcast.66, bf16[2048,768]{1,0:T(8,128)(2,1)S(1)} %get-tuple-element.698, f32[2048]{0:T(1024)S(1)} %get-tuple-element.696, f32[512]{0:T(512)S(1)} %dynamic_slice.127, f32[512]{0:T(512)S(1)} %dynamic-slice_negate_fusion.4, s32[2048]{0:T(1024)S(1)} %fusion.77, ...), kind=kOutput, calls=%fused_computation.4.clone.1 | convolution fusion | flops 1619000832 | bytes 8151044 | tf_op jit(solution)/shard_map/while/body/eval_jaxpr/dot_general | solution.py:62
  134.8 0.6 dynamic_slice.126
  137.9 2.4 broadcast_in_dim.65
  141.8 5.7 %fusion.78 = f32[512]{0:T(512)S(1)} fusion(f32[64,8,16,128]{3,2,1,0:T(8,128)} %bitcast.66, bf16[2048,768]{1,0:T(8,128)(2,1)S(1)} %get-tuple-element.698, f32[2048]{0:T(1024)S(1)} %get-tuple-element.696, f32[512]{0:T(512)S(1)} %dynamic_slice.127, f32[512]{0:T(512)S(1)} %dynamic-slice_negate_fusion.4, s32[2048]{0:T(1024)S(1)} %fusion.77, ...), kind=kOutput, calls=%fused_computation.4.clone.1 | convolution fusion | flops 1619000832 | bytes 8151044 | tf_op jit(solution)/shard_map/while/body/eval_jaxpr/dot_general | solution.py:62
  147.6 0.6 dynamic_slice.126
  150.7 2.4 broadcast_in_dim.65
  154.6 5.7 %fusion.78 = f32[512]{0:T(512)S(1)} fusion(f32[64,8,16,128]{3,2,1,0:T(8,128)} %bitcast.66, bf16[2048,768]{1,0:T(8,128)(2,1)S(1)} %get-tuple-element.698, f32[2048]{0:T(1024)S(1)} %get-tuple-element.696, f32[512]{0:T(512)S(1)} %dynamic_slice.127, f32[512]{0:T(512)S(1)} %dynamic-slice_negate_fusion.4, s32[2048]{0:T(1024)S(1)} %fusion.77, ...), kind=kOutput, calls=%fused_computation.4.clone.1 | convolution fusion | flops 1619000832 | bytes 8151044 | tf_op jit(solution)/shard_map/while/body/eval_jaxpr/dot_general | solution.py:62
  160.3 0.6 dynamic_slice.126
  163.4 2.4 broadcast_in_dim.65
  167.3 5.7 %fusion.78 = f32[512]{0:T(512)S(1)} fusion(f32[64,8,16,128]{3,2,1,0:T(8,128)} %bitcast.66, bf16[2048,768]{1,0:T(8,128)(2,1)S(1)} %get-tuple-element.698, f32[2048]{0:T(1024)S(1)} %get-tuple-element.696, f32[512]{0:T(512)S(1)} %dynamic_slice.127, f32[512]{0:T(512)S(1)} %dynamic-slice_negate_fusion.4, s32[2048]{0:T(1024)S(1)} %fusion.77, ...), kind=kOutput, calls=%fused_computation.4.clone.1 | convolution fusion | flops 1619000832 | bytes 8151044 | tf_op jit(solution)/shard_map/while/body/eval_jaxpr/dot_general | solution.py:62
  173.1 0.6 dynamic_slice.126
  176.2 2.4 broadcast_in_dim.65
  180.1 5.7 %fusion.78 = f32[512]{0:T(512)S(1)} fusion(f32[64,8,16,128]{3,2,1,0:T(8,128)} %bitcast.66, bf16[2048,768]{1,0:T(8,128)(2,1)S(1)} %get-tuple-element.698, f32[2048]{0:T(1024)S(1)} %get-tuple-element.696, f32[512]{0:T(512)S(1)} %dynamic_slice.127, f32[512]{0:T(512)S(1)} %dynamic-slice_negate_fusion.4, s32[2048]{0:T(1024)S(1)} %fusion.77, ...), kind=kOutput, calls=%fused_computation.4.clone.1 | convolution fusion | flops 1619000832 | bytes 8151044 | tf_op jit(solution)/shard_map/while/body/eval_jaxpr/dot_general | solution.py:62
  185.8 0.6 dynamic_slice.126
  188.9 2.4 broadcast_in_dim.65
  192.8 5.7 %fusion.78 = f32[512]{0:T(512)S(1)} fusion(f32[64,8,16,128]{3,2,1,0:T(8,128)} %bitcast.66, bf16[2048,768]{1,0:T(8,128)(2,1)S(1)} %get-tuple-element.698, f32[2048]{0:T(1024)S(1)} %get-tuple-element.696, f32[512]{0:T(512)S(1)} %dynamic_slice.127, f32[512]{0:T(512)S(1)} %dynamic-slice_negate_fusion.4, s32[2048]{0:T(1024)S(1)} %fusion.77, ...), kind=kOutput, calls=%fused_computation.4.clone.1 | convolution fusion | flops 1619000832 | bytes 8151044 | tf_op jit(solution)/shard_map/while/body/eval_jaxpr/dot_general | solution.py:62
  198.5 0.6 dynamic_slice.126
  201.6 2.4 broadcast_in_dim.65
  205.5 5.7 %fusion.78 = f32[512]{0:T(512)S(1)} fusion(f32[64,8,16,128]{3,2,1,0:T(8,128)} %bitcast.66, bf16[2048,768]{1,0:T(8,128)(2,1)S(1)} %get-tuple-element.698, f32[2048]{0:T(1024)S(1)} %get-tuple-element.696, f32[512]{0:T(512)S(1)} %dynamic_slice.127, f32[512]{0:T(512)S(1)} %dynamic-slice_negate_fusion.4, s32[2048]{0:T(1024)S(1)} %fusion.77, ...), kind=kOutput, calls=%fused_computation.4.clone.1 | convolution fusion | flops 1619000832 | bytes 8151044 | tf_op jit(solution)/shard_map/while/body/eval_jaxpr/dot_general | solution.py:62
  211.3 0.6 dynamic_slice.126
  214.4 2.4 broadcast_in_dim.65
  218.3 5.7 %fusion.78 = f32[512]{0:T(512)S(1)} fusion(f32[64,8,16,128]{3,2,1,0:T(8,128)} %bitcast.66, bf16[2048,768]{1,0:T(8,128)(2,1)S(1)} %get-tuple-element.698, f32[2048]{0:T(1024)S(1)} %get-tuple-element.696, f32[512]{0:T(512)S(1)} %dynamic_slice.127, f32[512]{0:T(512)S(1)} %dynamic-slice_negate_fusion.4, s32[2048]{0:T(1024)S(1)} %fusion.77, ...), kind=kOutput, calls=%fused_computation.4.clone.1 | convolution fusion | flops 1619000832 | bytes 8151044 | tf_op jit(solution)/shard_map/while/body/eval_jaxpr/dot_general | solution.py:62
  224.0 51.3 %psum.14 = f32[4096]{0:T(1024)S(1)} all-reduce(f32[4096]{0:T(1024)S(1)} %bitcast.69), channel_id=1, replica_groups=mesh['row'=8,'col'=16] {'col'}, use_global_device_ids=true, to_apply=%region_5.6 | all-reduce | flops 4096 | bytes 32768 | tf_op jit(solution)/shard_map/psum | solution.py:81
  275.4 19.4 %all-gather.2 = f32[8,1,256]{2,1,0:T(1,128)S(1)} all-gather(f32[1,1,256]{2,1,0:T(1,128)S(1)} %bitcast.75), channel_id=1, replica_groups=mesh['row'=8,'col'=16] {'row'}, dimensions={0}, use_global_device_ids=true | all-gather | bytes 9216 | tf_op jit(solution)/shard_map/all_gather | solution.py:83
  294.8 114.9 %while.27 = (s32[]{:T(128)}, f32[8,512,256]{2,1,0:T(8,128)}, s32[8]{0:T(128)S(1)}, s32[4096]{0:T(1024)S(1)}, f32[32,16]{1,0:T(8,128)S(1)}, /*index=5*/f32[4096]{...) while((s32[]{:T(128)}, f32[8,512,256]{2,1,0:T(8,128)}, ...), condition=%wide.region_7.8_spmd.clone, body=%wide.region_6.7_spmd.clone.sunk | while | flops 2162196992 | bytes 13960894 | solution.py:96
  294.8 0.6 dynamic_slice.132
  297.7 2.4 broadcast_in_dim.66
  301.6 7.6 %fusion.83 = f32[8,512,256]{2,1,0:T(8,128)} fusion(f32[8,512,256]{2,1,0:T(8,128)} %get-tuple-element.730, s32[]{:T(128)} %get-tuple-element.729, bf16[2048,256]{1,0:T(8,128)(2,1)} %get-tuple-element.764, f32[64,8,16,128]{3,2,1,0:T(8,128)} %bitcast.65, bf16[2048,768]{1,0:T(8,128)(2,1)S(1)} %get-tuple-element.760, f32[2048]{0:T(1024)S(1)} %get-tuple-element.763, ...), kind=kOutput, calls=%fused_computation.28.clone.1 | convolution fusion | flops 2162163712 | bytes 9740804 | tf_op jit(solution)/shard_map/while/body/eval_jaxpr/dot_general | solution.py:93
  309.2 0.6 dynamic_slice.132
  312.0 2.4 broadcast_in_dim.66
  315.9 7.6 %fusion.83 = f32[8,512,256]{2,1,0:T(8,128)} fusion(f32[8,512,256]{2,1,0:T(8,128)} %get-tuple-element.730, s32[]{:T(128)} %get-tuple-element.729, bf16[2048,256]{1,0:T(8,128)(2,1)} %get-tuple-element.764, f32[64,8,16,128]{3,2,1,0:T(8,128)} %bitcast.65, bf16[2048,768]{1,0:T(8,128)(2,1)S(1)} %get-tuple-element.760, f32[2048]{0:T(1024)S(1)} %get-tuple-element.763, ...), kind=kOutput, calls=%fused_computation.28.clone.1 | convolution fusion | flops 2162163712 | bytes 9740804 | tf_op jit(solution)/shard_map/while/body/eval_jaxpr/dot_general | solution.py:93
  323.5 0.6 dynamic_slice.132
  326.4 2.4 broadcast_in_dim.66
  330.3 7.6 %fusion.83 = f32[8,512,256]{2,1,0:T(8,128)} fusion(f32[8,512,256]{2,1,0:T(8,128)} %get-tuple-element.730, s32[]{:T(128)} %get-tuple-element.729, bf16[2048,256]{1,0:T(8,128)(2,1)} %get-tuple-element.764, f32[64,8,16,128]{3,2,1,0:T(8,128)} %bitcast.65, bf16[2048,768]{1,0:T(8,128)(2,1)S(1)} %get-tuple-element.760, f32[2048]{0:T(1024)S(1)} %get-tuple-element.763, ...), kind=kOutput, calls=%fused_computation.28.clone.1 | convolution fusion | flops 2162163712 | bytes 9740804 | tf_op jit(solution)/shard_map/while/body/eval_jaxpr/dot_general | solution.py:93
  337.9 0.6 dynamic_slice.132
  340.7 2.4 broadcast_in_dim.66
  344.6 7.6 %fusion.83 = f32[8,512,256]{2,1,0:T(8,128)} fusion(f32[8,512,256]{2,1,0:T(8,128)} %get-tuple-element.730, s32[]{:T(128)} %get-tuple-element.729, bf16[2048,256]{1,0:T(8,128)(2,1)} %get-tuple-element.764, f32[64,8,16,128]{3,2,1,0:T(8,128)} %bitcast.65, bf16[2048,768]{1,0:T(8,128)(2,1)S(1)} %get-tuple-element.760, f32[2048]{0:T(1024)S(1)} %get-tuple-element.763, ...), kind=kOutput, calls=%fused_computation.28.clone.1 | convolution fusion | flops 2162163712 | bytes 9740804 | tf_op jit(solution)/shard_map/while/body/eval_jaxpr/dot_general | solution.py:93
  352.2 0.6 dynamic_slice.132
  355.1 2.4 broadcast_in_dim.66
  359.0 7.6 %fusion.83 = f32[8,512,256]{2,1,0:T(8,128)} fusion(f32[8,512,256]{2,1,0:T(8,128)} %get-tuple-element.730, s32[]{:T(128)} %get-tuple-element.729, bf16[2048,256]{1,0:T(8,128)(2,1)} %get-tuple-element.764, f32[64,8,16,128]{3,2,1,0:T(8,128)} %bitcast.65, bf16[2048,768]{1,0:T(8,128)(2,1)S(1)} %get-tuple-element.760, f32[2048]{0:T(1024)S(1)} %get-tuple-element.763, ...), kind=kOutput, calls=%fused_computation.28.clone.1 | convolution fusion | flops 2162163712 | bytes 9740804 | tf_op jit(solution)/shard_map/while/body/eval_jaxpr/dot_general | solution.py:93
  369.5 2.4 broadcast_in_dim.66
  373.4 7.7 %fusion.83 = f32[8,512,256]{2,1,0:T(8,128)} fusion(f32[8,512,256]{2,1,0:T(8,128)} %get-tuple-element.730, s32[]{:T(128)} %get-tuple-element.729, bf16[2048,256]{1,0:T(8,128)(2,1)} %get-tuple-element.764, f32[64,8,16,128]{3,2,1,0:T(8,128)} %bitcast.65, bf16[2048,768]{1,0:T(8,128)(2,1)S(1)} %get-tuple-element.760, f32[2048]{0:T(1024)S(1)} %get-tuple-element.763, ...), kind=kOutput, calls=%fused_computation.28.clone.1 | convolution fusion | flops 2162163712 | bytes 9740804 | tf_op jit(solution)/shard_map/while/body/eval_jaxpr/dot_general | solution.py:93
  383.9 2.4 broadcast_in_dim.66
  387.8 7.6 %fusion.83 = f32[8,512,256]{2,1,0:T(8,128)} fusion(f32[8,512,256]{2,1,0:T(8,128)} %get-tuple-element.730, s32[]{:T(128)} %get-tuple-element.729, bf16[2048,256]{1,0:T(8,128)(2,1)} %get-tuple-element.764, f32[64,8,16,128]{3,2,1,0:T(8,128)} %bitcast.65, bf16[2048,768]{1,0:T(8,128)(2,1)S(1)} %get-tuple-element.760, f32[2048]{0:T(1024)S(1)} %get-tuple-element.763, ...), kind=kOutput, calls=%fused_computation.28.clone.1 | convolution fusion | flops 2162163712 | bytes 9740804 | tf_op jit(solution)/shard_map/while/body/eval_jaxpr/dot_general | solution.py:93
  398.2 2.4 broadcast_in_dim.66
  402.1 7.6 %fusion.83 = f32[8,512,256]{2,1,0:T(8,128)} fusion(f32[8,512,256]{2,1,0:T(8,128)} %get-tuple-element.730, s32[]{:T(128)} %get-tuple-element.729, bf16[2048,256]{1,0:T(8,128)(2,1)} %get-tuple-element.764, f32[64,8,16,128]{3,2,1,0:T(8,128)} %bitcast.65, bf16[2048,768]{1,0:T(8,128)(2,1)S(1)} %get-tuple-element.760, f32[2048]{0:T(1024)S(1)} %get-tuple-element.763, ...), kind=kOutput, calls=%fused_computation.28.clone.1 | convolution fusion | flops 2162163712 | bytes 9740804 | tf_op jit(solution)/shard_map/while/body/eval_jaxpr/dot_general | solution.py:93
  409.7 130.2 %all-reduce.2.cloned.1.call-done = f32[4096,256]{1,0:T(8,128)} async-done(((f32[4096,256]{1,0:T(8,128)}), f32[4096,256]{1,0:T(8,128)}) %all-reduce.2.cloned.1.call-update) | async-done | bytes 4194320 | tf_op jit(solution)/shard_map/psum | solution.py:97
  539.9 1.7 constant_dynamic-slice_fusion.2
  (121 shorter events, 7.4 us)
Async XLA Ops:
  6.5 68.8 %all-gather.9.cloned.1.call-start = ((), (), s32[]{:S(2)}) async-start(), calls=%async_computation.1 | async-start | bytes 3538944 | tf_op jit(solution)/shard_map/all_gather | solution.py:35
  7.3 110.6 %all-gather.7.cloned.1.call-start = ((), (), s32[]{:S(2)}) async-start(), calls=%async_computation | async-start | bytes 6684672 | tf_op jit(solution)/shard_map/all_gather | solution.py:31
  8.0 286.8 %all-gather.11.cloned.1.call-start = ((), (), s32[]{:S(2)}) async-start(), calls=%async_computation.2 | async-start | bytes 1179648 | tf_op jit(solution)/shard_map/all_gather | solution.py:37
  8.7 531.2 %all-reduce.2.cloned.1.call-start = ((), (), s32[]{:S(2)}) async-start(), calls=%async_computation.3 | async-start | bytes 8388608 | tf_op jit(solution)/shard_map/psum | solution.py:97
  75.3 46.6 %copy-start = (bf16[2048,768]{1,0:T(8,128)(2,1)S(1)}, bf16[2048,768]{1,0:T(8,128)(2,1)}, u32[]{:S(2)}) copy-start(bf16[2048,768]{1,0:T(8,128)(2,1)} %all-gather.9.cloned.1.call-done) | copy-start | bytes 9437188
Sparse Core Ops, SparseCore 0:
  9.7 65.6 all-gather.8
  77.0 40.7 all-gather.6
  120.2 45.7 all-gather.10
  409.9 130.0 all-reduce.1
where the time goes:
time: 549 us; the launch traced here: 548 us
  waiting for transfers between devices  193 us (35%)
  blocking collectives  112 us (20%)
  matrix products  109 us (20%)
  loops' own time  57.7 us (11%)
  local copies, waits for them, and re-layouts  54 us (10%)
  between operations  13.2 us (2%)
  other arithmetic  8.3 us (2%)
    psum x1, waiting for transfers between devices, shards(): summed = lax.psum(partial_out, 'col')  130 us
    dot_general x8, matrix products, one_block(): return jnp.dot(weight, cols_feat, preferred_element_type=jnp.float32)  61 us
    psum x1, blocking collectives, shards(): row_totals = lax.psum(row_partial, 'col')  51.3 us
    dot_general x8, matrix products, block_terms(): lax.dot_general(row_emb, cols_x, (((1,), (1,)), ((), ())), preferred_elem...  45.4 us
    all_gather x1, waiting for transfers between devices, shards(): lax.all_gather(embeddings, 'col', axis=0, tiled=True)  39.8 us
    broadcast_in_dim x16, local copies, waits for them, and re-layouts, block_terms(): jnp.broadcast_to(active_part[:, None, :, None], (size // BLK, BLK, col_bl...  38.6 us
    another operation x1, loops' own time, shards(): lax.map(lambda start: jnp.sum(block_terms(start, block_rows)[2], axis=1),...  30.1 us
    another operation x1, loops' own time, shards(): lax.map(one_block, begins).reshape(total_rows, cols_feat.shape[1])  27.6 us
  transfers between devices with their start and end apart: 4, of which 3 were waited for; matrix products, arithmetic and copies ran while one was open for 15% of the time, Pallas kernels for 0%

commit v1 on v0

--- a/solution.py
+++ b/solution.py
@@ -28,7 +28,9 @@
 
 def shards(embeddings, spread, features, block_list, list_pairs):
     rows_x, rows_beta = (
-        lax.all_gather(embeddings, "col", axis=0, tiled=True),
+        jnp.concatenate(
+            lax.all_to_all(jnp.stack([embeddings] * lax.axis_size("col")), "col", 0, 0), axis=0
+        ),
         lax.all_gather(spread, "col", axis=0, tiled=True),
     )
     cols_x, cols_beta, cols_feat = (

time: 549 us -> 592 us (1.078)
  blocking collectives: 112 us -> 204 us
  waiting for transfers between devices: 193 us -> 134 us
  starting transfers between devices: 0.12 us -> 7.12 us
    all_gather x1, blocking collectives: 21.2 us -> 115 us  [shards(): lax.all_gather(spread, 'col', axis=0, tiled=True)]
    all_gather x1 -> x0, waiting for transfers between devices: 39.8 us -> none  [shards(): lax.all_gather(embeddings, 'col', axis=0, tiled=True)]
    all_gather x1, waiting for transfers between devices: 21 us -> 0.02 us  [shards(): lax.all_gather(embeddings, 'row', axis=0, tiled=True)]
    all_to_all x0 -> x1, starting transfers between devices: none -> 7.05 us  [shards(): lax.all_to_all(jnp.stack([embeddings] * lax.axis_size('col')), 'col', 0, 0)]
  transfers between devices with their start and end apart: 4 -> 4, of which waited for: 3 -> 1; matrix products, arithmetic and copies ran while one was open for 15% -> 14% of each run, Pallas kernels for 0% -> 0%
where the time goes in v1:
time: 592 us; the launch traced here: 590 us
  blocking collectives  204 us (34%)
  waiting for transfers between devices  134 us (23%)
  matrix products  107 us (18%)
  loops' own time  59.3 us (10%)
  local copies, waits for them, and re-layouts  57.5 us (10%)
  between operations  13.3 us (2%)
  other arithmetic  8.29 us (1%)
  starting transfers between devices  7.12 us (1%)
    psum x1, waiting for transfers between devices, shards(): summed = lax.psum(partial_out, 'col')  133 us
    all_gather x1, blocking collectives, shards(): lax.all_gather(spread, 'col', axis=0, tiled=True)  115 us
    dot_general x8, matrix products, one_block(): return jnp.dot(weight, cols_feat, preferred_element_type=jnp.float32)  60.9 us
    psum x1, blocking collectives, shards(): row_totals = lax.psum(row_partial, 'col')  52.4 us
    dot_general x8, matrix products, block_terms(): lax.dot_general(row_emb, cols_x, (((1,), (1,)), ((), ())), preferred_elem...  45.2 us
    broadcast_in_dim x16, local copies, waits for them, and re-layouts, block_terms(): jnp.broadcast_to(active_part[:, None, :, None], (size // BLK, BLK, col_bl...  37.7 us
    another operation x1, loops' own time, shards(): lax.map(lambda start: jnp.sum(block_terms(start, block_rows)[2], axis=1),...  29.8 us
    another operation x1, loops' own time, shards(): lax.map(one_block, begins).reshape(total_rows, cols_feat.shape[1])  29.6 us
  transfers between devices with their start and end apart: 4, of which 1 were waited for; matrix products, arithmetic and copies ran while one was open for 14% of the time, Pallas kernels for 0%

profile of v1, /device:TPU:1, one launch (start us, length us, event | category | flops | bytes accessed | tf_op | source)
XLA Modules:
  0.0 590.4 jit_solution(5398249389695579258)
XLA Ops:
  6.5 0.7 all-gather.6.cloned.1.call-update
  7.3 4.3 stack.2
  11.5 7.0 %all-to-all-start = ((bf16[16,256,768]{2,1,0:T(8,128)(2,1)}), bf16[16,256,768]{2,1,0:T(8,128)(2,1)}, u32[]{:S(2)}, u32[]{:S(2)}) async-start(bf16[16,256,768]{2,1,0:T(8,128)(2,1)} %stack.2), calls=%async_computation | async-start | bytes 12582912 | tf_op jit(solution)/shard_map/all_to_all | solution.py:32
  18.6 0.7 all-gather.8.cloned.1.call-update
  19.7 115.4 %all-gather = bf16[16,1,256]{2,1,0:T(2,128)(2,1)S(1)} all-gather(bf16[1,1,256]{2,1,0:T(2,128)(2,1)S(1)} %reshape.51), channel_id=1, replica_groups=mesh['row'=8,'col'=16] {'col'}, dimensions={0}, use_global_device_ids=true | all-gather | bytes 8704 | tf_op jit(solution)/shard_map/all_gather | solution.py:34
  135.0 21.0 %all-gather.1 = bf16[8,1,256]{2,1,0:T(2,128)(2,1)S(1)} all-gather(bf16[1,1,256]{2,1,0:T(2,128)(2,1)S(1)} %reshape.51), channel_id=1, replica_groups=mesh['row'=8,'col'=16] {'row'}, dimensions={0}, use_global_device_ids=true | all-gather | bytes 4608 | tf_op jit(solution)/shard_map/all_gather | solution.py:38
  156.1 0.2 fusion.40
  156.3 0.2 fusion.41
  156.9 2.7 multiply_reduce_fusion.1
  159.6 4.1 multiply_reduce_fusion
  163.7 101.3 %while.26 = (s32[]{:T(128)}, f32[8,512]{1,0:T(8,128)S(1)}, s32[8]{0:T(128)S(1)}, s32[4096]{0:T(1024)S(1)}, f32[32,16]{1,0:T(8,128)S(1)}, /*index=5*/f32[4096]{0:...) while((s32[]{:T(128)}, f32[8,512]{1,0:T(8,128)S(1)}, ...), condition=%wide.region_4.5_spmd.clone, body=%wide.region_2.4_spmd.clone.sunk | while | flops 1619034112 | bytes 12371102 | solution.py:80
  163.8 0.6 dynamic_slice.126
  166.9 2.4 broadcast_in_dim.65
  170.7 5.7 fusion.78
  176.4 0.6 dynamic_slice.126
  179.5 2.4 broadcast_in_dim.65
  183.4 5.7 fusion.78
  189.1 0.6 dynamic_slice.126
  192.2 2.4 broadcast_in_dim.65
  196.0 5.6 fusion.78
  201.7 0.6 dynamic_slice.126
  204.8 2.4 broadcast_in_dim.65
  208.7 5.6 fusion.78
  214.4 0.6 dynamic_slice.126
  217.5 2.4 broadcast_in_dim.65
  221.3 5.6 fusion.78
  227.1 0.6 dynamic_slice.126
  230.2 2.4 broadcast_in_dim.65
  234.0 5.6 fusion.78
  239.7 0.6 dynamic_slice.126
  242.8 2.4 broadcast_in_dim.65
  246.6 5.6 fusion.78
  252.4 0.6 dynamic_slice.126
  255.5 2.4 broadcast_in_dim.65
  259.3 5.6 fusion.78
  265.0 52.4 %psum.14 = f32[4096]{0:T(1024)S(1)} all-reduce(f32[4096]{0:T(1024)S(1)} %bitcast.74), channel_id=1, replica_groups=mesh['row'=8,'col'=16] {'col'}, use_global_device_ids=true, to_apply=%region_5.6 | all-reduce | flops 4096 | bytes 32768 | tf_op jit(solution)/shard_map/psum | solution.py:83
  317.5 14.8 %all-gather.2 = f32[8,1,256]{2,1,0:T(1,128)S(1)} all-gather(f32[1,1,256]{2,1,0:T(1,128)S(1)} %bitcast.80), channel_id=1, replica_groups=mesh['row'=8,'col'=16] {'row'}, dimensions={0}, use_global_device_ids=true | all-gather | bytes 9216 | tf_op jit(solution)/shard_map/all_gather | solution.py:85
  332.3 116.9 %while.27 = (s32[]{:T(128)}, f32[8,512,256]{2,1,0:T(8,128)}, s32[8]{0:T(128)S(1)}, s32[4096]{0:T(1024)S(1)}, f32[32,16]{1,0:T(8,128)S(1)}, /*index=5*/f32[4096]{...) while((s32[]{:T(128)}, f32[8,512,256]{2,1,0:T(8,128)}, ...), condition=%wide.region_7.8_spmd.clone, body=%wide.region_6.7_spmd.clone.sunk | while | flops 2162196992 | bytes 13960894 | solution.py:98
  332.3 0.6 dynamic_slice.132
  335.4 2.4 broadcast_in_dim.66
  339.3 7.6 %fusion.83 = f32[8,512,256]{2,1,0:T(8,128)} fusion(f32[8,512,256]{2,1,0:T(8,128)} %get-tuple-element.730, s32[]{:T(128)} %get-tuple-element.729, bf16[2048,256]{1,0:T(8,128)(2,1)} %get-tuple-element.764, f32[64,8,16,128]{3,2,1,0:T(8,128)} %bitcast.68, bf16[2048,768]{1,0:T(8,128)(2,1)S(1)} %get-tuple-element.760, f32[2048]{0:T(1024)S(1)} %get-tuple-element.763, ...), kind=kOutput, calls=%fused_computation.28.clone.1 | convolution fusion | flops 2162163712 | bytes 9740804 | tf_op jit(solution)/shard_map/while/body/eval_jaxpr/dot_general | solution.py:95
  346.9 0.6 dynamic_slice.132
  350.0 2.4 broadcast_in_dim.66
  353.9 7.6 %fusion.83 = f32[8,512,256]{2,1,0:T(8,128)} fusion(f32[8,512,256]{2,1,0:T(8,128)} %get-tuple-element.730, s32[]{:T(128)} %get-tuple-element.729, bf16[2048,256]{1,0:T(8,128)(2,1)} %get-tuple-element.764, f32[64,8,16,128]{3,2,1,0:T(8,128)} %bitcast.68, bf16[2048,768]{1,0:T(8,128)(2,1)S(1)} %get-tuple-element.760, f32[2048]{0:T(1024)S(1)} %get-tuple-element.763, ...), kind=kOutput, calls=%fused_computation.28.clone.1 | convolution fusion | flops 2162163712 | bytes 9740804 | tf_op jit(solution)/shard_map/while/body/eval_jaxpr/dot_general | solution.py:95
  361.6 0.6 dynamic_slice.132
  364.7 2.4 broadcast_in_dim.66
  368.6 7.6 %fusion.83 = f32[8,512,256]{2,1,0:T(8,128)} fusion(f32[8,512,256]{2,1,0:T(8,128)} %get-tuple-element.730, s32[]{:T(128)} %get-tuple-element.729, bf16[2048,256]{1,0:T(8,128)(2,1)} %get-tuple-element.764, f32[64,8,16,128]{3,2,1,0:T(8,128)} %bitcast.68, bf16[2048,768]{1,0:T(8,128)(2,1)S(1)} %get-tuple-element.760, f32[2048]{0:T(1024)S(1)} %get-tuple-element.763, ...), kind=kOutput, calls=%fused_computation.28.clone.1 | convolution fusion | flops 2162163712 | bytes 9740804 | tf_op jit(solution)/shard_map/while/body/eval_jaxpr/dot_general | solution.py:95
  376.2 0.6 dynamic_slice.132
  379.3 2.4 broadcast_in_dim.66
  383.2 7.6 %fusion.83 = f32[8,512,256]{2,1,0:T(8,128)} fusion(f32[8,512,256]{2,1,0:T(8,128)} %get-tuple-element.730, s32[]{:T(128)} %get-tuple-element.729, bf16[2048,256]{1,0:T(8,128)(2,1)} %get-tuple-element.764, f32[64,8,16,128]{3,2,1,0:T(8,128)} %bitcast.68, bf16[2048,768]{1,0:T(8,128)(2,1)S(1)} %get-tuple-element.760, f32[2048]{0:T(1024)S(1)} %get-tuple-element.763, ...), kind=kOutput, calls=%fused_computation.28.clone.1 | convolution fusion | flops 2162163712 | bytes 9740804 | tf_op jit(solution)/shard_map/while/body/eval_jaxpr/dot_general | solution.py:95
  390.8 0.6 dynamic_slice.132
  393.8 2.4 broadcast_in_dim.66
  397.7 7.6 %fusion.83 = f32[8,512,256]{2,1,0:T(8,128)} fusion(f32[8,512,256]{2,1,0:T(8,128)} %get-tuple-element.730, s32[]{:T(128)} %get-tuple-element.729, bf16[2048,256]{1,0:T(8,128)(2,1)} %get-tuple-element.764, f32[64,8,16,128]{3,2,1,0:T(8,128)} %bitcast.68, bf16[2048,768]{1,0:T(8,128)(2,1)S(1)} %get-tuple-element.760, f32[2048]{0:T(1024)S(1)} %get-tuple-element.763, ...), kind=kOutput, calls=%fused_computation.28.clone.1 | convolution fusion | flops 2162163712 | bytes 9740804 | tf_op jit(solution)/shard_map/while/body/eval_jaxpr/dot_general | solution.py:95
  405.4 0.6 dynamic_slice.132
  408.5 2.4 broadcast_in_dim.66
  412.4 7.6 %fusion.83 = f32[8,512,256]{2,1,0:T(8,128)} fusion(f32[8,512,256]{2,1,0:T(8,128)} %get-tuple-element.730, s32[]{:T(128)} %get-tuple-element.729, bf16[2048,256]{1,0:T(8,128)(2,1)} %get-tuple-element.764, f32[64,8,16,128]{3,2,1,0:T(8,128)} %bitcast.68, bf16[2048,768]{1,0:T(8,128)(2,1)S(1)} %get-tuple-element.760, f32[2048]{0:T(1024)S(1)} %get-tuple-element.763, ...), kind=kOutput, calls=%fused_computation.28.clone.1 | convolution fusion | flops 2162163712 | bytes 9740804 | tf_op jit(solution)/shard_map/while/body/eval_jaxpr/dot_general | solution.py:95
  420.0 0.6 dynamic_slice.132
  423.1 2.4 broadcast_in_dim.66
  427.0 7.6 %fusion.83 = f32[8,512,256]{2,1,0:T(8,128)} fusion(f32[8,512,256]{2,1,0:T(8,128)} %get-tuple-element.730, s32[]{:T(128)} %get-tuple-element.729, bf16[2048,256]{1,0:T(8,128)(2,1)} %get-tuple-element.764, f32[64,8,16,128]{3,2,1,0:T(8,128)} %bitcast.68, bf16[2048,768]{1,0:T(8,128)(2,1)S(1)} %get-tuple-element.760, f32[2048]{0:T(1024)S(1)} %get-tuple-element.763, ...), kind=kOutput, calls=%fused_computation.28.clone.1 | convolution fusion | flops 2162163712 | bytes 9740804 | tf_op jit(solution)/shard_map/while/body/eval_jaxpr/dot_general | solution.py:95
  434.6 0.6 dynamic_slice.132
  437.7 2.4 broadcast_in_dim.66
  441.6 7.6 %fusion.83 = f32[8,512,256]{2,1,0:T(8,128)} fusion(f32[8,512,256]{2,1,0:T(8,128)} %get-tuple-element.730, s32[]{:T(128)} %get-tuple-element.729, bf16[2048,256]{1,0:T(8,128)(2,1)} %get-tuple-element.764, f32[64,8,16,128]{3,2,1,0:T(8,128)} %bitcast.68, bf16[2048,768]{1,0:T(8,128)(2,1)S(1)} %get-tuple-element.760, f32[2048]{0:T(1024)S(1)} %get-tuple-element.763, ...), kind=kOutput, calls=%fused_computation.28.clone.1 | convolution fusion | flops 2162163712 | bytes 9740804 | tf_op jit(solution)/shard_map/while/body/eval_jaxpr/dot_general | solution.py:95
  449.2 133.0 %all-reduce.2.cloned.1.call-done = f32[4096,256]{1,0:T(8,128)} async-done(((f32[4096,256]{1,0:T(8,128)}), f32[4096,256]{1,0:T(8,128)}) %all-reduce.2.cloned.1.call-update) | async-done | bytes 4194320 | tf_op jit(solution)/shard_map/psum | solution.py:99
  582.2 1.7 constant_dynamic-slice_fusion.2
  (128 shorter events, 5.9 us)
Async XLA Ops:
  6.5 150.3 %all-gather.6.cloned.1.call-start = ((), (), s32[]{:S(2)}) async-start(), calls=%async_computation.1 | async-start | bytes 3538944 | tf_op jit(solution)/shard_map/all_gather | solution.py:37
  11.5 8.1 %copy-start.3 = (bf16[256]{0:T(256)(128)(2,1)S(1)}, bf16[256]{0:T(256)(128)(2,1)}, u32[]{:S(2)}) copy-start(bf16[256]{0:T(256)(128)(2,1)} %param.10) | copy-start | bytes 1540
  11.5 144.6 %copy-start.2 = (s32[256]{0:T(256)S(1)}, s32[256]{0:T(256)}, u32[]{:S(2)}) copy-start(s32[256]{0:T(256)} %param.12) | copy-start | bytes 3076
  11.5 145.0 %copy-start.1 = (s32[64,64]{1,0:T(8,128)S(1)}, s32[64,64]{1,0:T(8,128)}, u32[]{:S(2)}) copy-start(s32[64,64]{1,0:T(8,128)} %param.13) | copy-start | bytes 49156
  11.5 148.1 %all-to-all-start = ((bf16[16,256,768]{2,1,0:T(8,128)(2,1)}), bf16[16,256,768]{2,1,0:T(8,128)(2,1)}, u32[]{:S(2)}, u32[]{:S(2)}) async-start(bf16[16,256,768]{2,1,0:T(8,128)(2,1)} %stack.2), calls=%async_computation | async-start | bytes 12582912 | tf_op jit(solution)/shard_map/all_to_all | solution.py:32
  18.6 313.8 %all-gather.8.cloned.1.call-start = ((), (), s32[]{:S(2)}) async-start(), calls=%async_computation.2 | async-start | bytes 1179648 | tf_op jit(solution)/shard_map/all_gather | solution.py:39
  19.3 562.9 %all-reduce.2.cloned.1.call-start = ((), (), s32[]{:S(2)}) async-start(), calls=%async_computation.3 | async-start | bytes 8388608 | tf_op jit(solution)/shard_map/psum | solution.py:99
  156.9 6.9 %copy-start = (bf16[2048,768]{1,0:T(8,128)(2,1)S(1)}, bf16[2048,768]{1,0:T(8,128)(2,1)}, u32[]{:S(2)}) copy-start(bf16[2048,768]{1,0:T(8,128)(2,1)} %all-gather.6.cloned.1.call-done) | copy-start | bytes 9437188
Sparse Core Ops, SparseCore 0:
  9.7 87.4 all-gather.5
  99.5 44.2 all-gather.7
  449.3 132.8 all-reduce.1
